TPU v7x, 32 devices: a whole 2x2x4 slice. The times are simulated.
32 devices in a mesh: shot: 2 (over x), gx: 16 (over z, y, core).
Axes of the slice: x: 2, y: 2, z: 4, core: 2. Of those that a mesh axis runs over, the one named last changes fastest.
Arguments:
- waves_now: float32 [2, 1024, 64, 128], P(None, ('shot', 'gx')), parts along dimension 1, may hold values from -6 to 6
- waves_prev: float32 [2, 1024, 64, 128], P(None, ('shot', 'gx')), parts along dimension 1, may hold values from -6 to 6
- epsilon: bfloat16 [512, 64, 128], P('gx'), may hold values from 0.049804688 to 0.3984375
- tilt: bfloat16 [512, 64, 128], P('gx'), may hold values from -3.140625 to 3.140625
- azimuth: bfloat16 [512, 64, 128], P('gx'), may hold values from -3.140625 to 3.140625
- courant: bfloat16 [512, 64, 128], P('gx'), may hold values from 0.029907227 to 0.099609375
- lag_offsets: int32 [32], replicated, may hold values from -16 to 15
- table_index: int32 [128], replicated, may hold values from 0 to 3
- lag_tables: bfloat16 [4, 32, 32], replicated, may hold values from -1 to 1
Outputs:
- angle_image: bfloat16 [32, 8192, 256], P(None, ('shot', 'gx')), parts along dimension 1
There are 2 independent parts, one for each index of `shot`. A program takes and returns all parts, laid end to end along the dimension named above; an argument that names none is the same for every part. Nothing has to cross between parts.
All inputs are finite; a program needn't handle non-finite values.
Results may differ from a plain program's by a relative error of at most 0.0049.
Values may be sent and summed in bfloat16 or wider, within the bound.
A program may use at most 64 MiB of HBM per device.

v0:
```python
import functools
import jax
import jax.numpy as jnp
from jax import lax
from jax.experimental import pallas as pl
from jax.experimental.pallas import tpu as pltpu
from jax.sharding import PartitionSpec as P

STEPS = 4
LAG_REACH = 16
PAD = 8
F32 = jnp.float32
SEND = jnp.float32


def sin_cos(x):
    h = x * 0.5
    h2 = h * h
    s = h2 * (-1.0 / 39916800.0) + (1.0 / 362880.0)
    s = s * h2 + (-1.0 / 5040.0)
    s = s * h2 + (1.0 / 120.0)
    s = s * h2 + (-1.0 / 6.0)
    s = s * h2 * h + h
    c = h2 * (1.0 / 479001600.0) + (-1.0 / 3628800.0)
    c = c * h2 + (1.0 / 40320.0)
    c = c * h2 + (-1.0 / 720.0)
    c = c * h2 + (1.0 / 24.0)
    c = c * h2 + (-0.5)
    c = c * h2 + 1.0
    s2 = s + s
    return s2 * c, 1.0 - s2 * s


def wave_kernel(
    n, jr, cols_per, now_hbm, prev_hbm, eps_hbm, tilt_hbm, azi_hbm, cou_hbm, cols_ref,
    buf0, buf1, dz, sz, dy, eps, tilt, azi, cou, coef, pair, snap, sendbuf, halo,
    in_sems, hs_sems, hr_sems, as_sems, ar_sems,
):
    width = eps.shape[0]
    ny = eps.shape[1]
    nz = eps.shape[2]
    rows = pl.ds(PAD, ny)
    up_rows = pl.ds(PAD + 1, ny)
    dn_rows = pl.ds(PAD - 1, ny)
    me = lax.axis_index("gx")
    has_low = me > 0
    has_high = me < n - 1
    bufs = (buf0, buf1)

    copies = [
        pltpu.make_async_copy(tilt_hbm, tilt, in_sems.at[0]),
        pltpu.make_async_copy(azi_hbm, azi, in_sems.at[1]),
        pltpu.make_async_copy(eps_hbm, eps, in_sems.at[2]),
        pltpu.make_async_copy(cou_hbm, cou, in_sems.at[3]),
        pltpu.make_async_copy(now_hbm, buf0.at[:, pl.ds(1, width), rows, :], in_sems.at[4]),
        pltpu.make_async_copy(prev_hbm, buf1.at[:, pl.ds(1, width), rows, :], in_sems.at[5]),
    ]
    for copy in copies:
        copy.start()

    barrier = pltpu.get_barrier_semaphore()

    def greet(k, carry):
        pl.semaphore_signal(
            barrier, inc=1, device_id={"gx": lax.rem(me + k, n)},
            device_id_type=pl.DeviceIdType.MESH,
        )
        return carry

    lax.fori_loop(1, n, greet, 0)

    zero_rows = jnp.zeros((2, width + 2, PAD, nz), F32)
    for ref in (buf0, buf1, dz):
        ref[:, :, pl.ds(0, PAD), :] = zero_rows
        ref[:, :, pl.ds(PAD + ny, PAD), :] = zero_rows
    zero_plane = jnp.zeros((2, ny, nz), F32)
    for ref in (buf0, buf1, dz, dy):
        for plane in (0, width + 1):
            ref[:, plane, rows, :] = zero_plane

    pl.semaphore_wait(barrier, n - 1)

    def halo_copy(step, side):
        if step == 0:
            src = now_hbm.at[:, 0 if side == 0 else width - 1]
        else:
            src = sendbuf.at[step - 1, side]
        return pltpu.make_async_remote_copy(
            src_ref=src,
            dst_ref=halo.at[step, 1 - side],
            send_sem=hs_sems.at[step, side],
            recv_sem=hr_sems.at[step, 1 - side],
            device_id={"gx": me - 1 if side == 0 else me + 1},
            device_id_type=pl.DeviceIdType.MESH,
        )

    def halo_arrived(step, side):
        return pltpu.make_async_remote_copy(
            src_ref=sendbuf.at[0, side],
            dst_ref=halo.at[step, side],
            send_sem=hs_sems.at[step, side],
            recv_sem=hr_sems.at[step, side],
            device_id={"gx": me - 1 if side == 0 else me + 1},
            device_id_type=pl.DeviceIdType.MESH,
        )

    def send_halo(step):
        @pl.when(has_low)
        def _():
            halo_copy(step, 0).start()

        @pl.when(has_high)
        def _():
            halo_copy(step, 1).start()

    send_halo(0)

    for copy in copies[:4]:
        copy.wait()

    def make_coef(x, carry):
        theta_s, theta_c = sin_cos(tilt[x].astype(F32))
        alpha_s, alpha_c = sin_cos(azi[x].astype(F32))
        speed = cou[x].astype(F32)
        e2 = eps[x].astype(F32) * 2.0
        scaled = speed * e2
        base = speed + scaled
        nx = theta_s * alpha_c
        nyy = theta_s * alpha_s
        sx = scaled * nx
        sy = scaled * nyy
        scz = scaled * theta_c
        mxx = base - sx * nx
        myy = base - sy * nyy
        mzz = base - scz * theta_c
        coef[0, x] = mxx
        coef[1, x] = myy
        coef[2, x] = mzz
        coef[3, x] = -0.5 * (sx * nyy)
        coef[4, x] = -0.5 * (scz * nx)
        coef[5, x] = -0.5 * (scz * nyy)
        coef[6, x] = 2.0 - 2.0 * (mxx + myy + mzz)
        return carry

    lax.fori_loop(0, width, make_coef, 0)
    for copy in copies[4:]:
        copy.wait()

    lane = lax.broadcasted_iota(jnp.int32, (ny, nz), 1)
    first = lane == 0
    last = lane == nz - 1

    def z_values(p):
        up = jnp.where(last, 0.0, pltpu.roll(p, nz - 1, axis=1))
        dn = jnp.where(first, 0.0, pltpu.roll(p, 1, axis=1))
        return up - dn, up + dn

    def z_pass(now, x):
        for f in range(2):
            d, s = z_values(now[f, x, rows, :])
            diff = now[f, x, up_rows, :] - now[f, x, dn_rows, :]
            dz[f, x, rows, :] = d
            sz[f, x] = s
            dy[f, x, rows, :] = diff

    def update(now, prv, x):
        c = [coef[k, x - 1] for k in range(7)]
        out = []
        for f in range(2):
            acc = c[6] * now[f, x, rows, :] - prv[f, x, rows, :]
            acc += c[0] * (now[f, x + 1, rows, :] + now[f, x - 1, rows, :])
            acc += c[1] * (now[f, x, up_rows, :] + now[f, x, dn_rows, :])
            acc += c[2] * sz[f, x]
            acc += c[3] * (dy[f, x + 1, rows, :] - dy[f, x - 1, rows, :])
            acc += c[4] * (dz[f, x + 1, rows, :] - dz[f, x - 1, rows, :])
            acc += c[5] * (dz[f, x, up_rows, :] - dz[f, x, dn_rows, :])
            out.append(acc)
        for f in range(2):
            prv[f, x, rows, :] = out[f]
        return out

    for step in range(STEPS):
        now, prv = bufs[step % 2], bufs[(step + 1) % 2]
        z_pass(now, 1)
        z_pass(now, 2)
        z_pass(now, 3)

        def interior(x, carry, now=now, prv=prv):
            update(now, prv, x)
            z_pass(now, x + 2)
            return carry

        lax.fori_loop(2, width - 1, interior, 0)
        update(now, prv, width - 1)

        for side, plane, edge, has in (
            (0, 0, 1, has_low), (1, width + 1, width, has_high),
        ):
            @pl.when(has)
            def _(side=side, plane=plane, now=now, step=step):
                halo_arrived(step, side).wait_recv()
                for f in range(2):
                    p = halo[step, side, f]
                    now[f, plane, rows, :] = p
                    d, _ = z_values(p)
                    dz[f, plane, rows, :] = d
                for f in range(2):
                    dy[f, plane, rows, :] = now[f, plane, up_rows, :] - now[f, plane, dn_rows, :]

            out = update(now, prv, edge)
            if step < STEPS - 1:
                for f in range(2):
                    sendbuf[step, side, f] = out[f]

                @pl.when(has)
                def _(side=side, step=step):
                    halo_copy(step + 1, side).start()

    final = bufs[STEPS % 2]
    half = width // 2

    def make_snap(i, carry):
        for f in range(2):
            pair[f] = final[f, 2 * i + 1, rows, :] + final[f, 2 * i + 2, rows, :]
        for f in range(2):
            even = pair[f, pl.ds(0, ny // 2, stride=2), :]
            odd = pair[f, pl.ds(1, ny // 2, stride=2), :]
            snap[f, pl.ds(i, ny // 2, stride=half), :] = (even + odd) * 0.25
        return carry

    lax.fori_loop(0, half, make_snap, 0)

    span = jr * half

    def piece(target, source):
        start = pl.multiple_of(((target * cols_per) // nz) * half, half)
        return pltpu.make_async_remote_copy(
            src_ref=snap.at[:, pl.ds(start, span), :],
            dst_ref=cols_ref.at[source],
            send_sem=as_sems.at[target],
            recv_sem=ar_sems.at[source],
            device_id={"gx": target},
            device_id_type=pl.DeviceIdType.MESH,
        )

    def send_piece(k, carry):
        piece(lax.rem(me + k, n), me).start()
        return carry

    lax.fori_loop(1, n, send_piece, 0)
    start = pl.multiple_of(((me * cols_per) // nz) * half, half)
    own = pltpu.make_async_copy(snap.at[:, pl.ds(start, span), :], cols_ref.at[me], in_sems.at[6])
    own.start()

    for step in range(STEPS):
        @pl.when(has_low)
        def _(step=step):
            halo_copy(step, 0).wait_send()

        @pl.when(has_high)
        def _(step=step):
            halo_copy(step, 1).wait_send()

    def wait_piece(k, carry):
        piece(lax.rem(me + k, n), me).wait_send()
        piece(lax.rem(me + k, n), lax.rem(me + k, n)).wait_recv()
        return carry

    lax.fori_loop(1, n, wait_piece, 0)
    own.wait()


def image_kernel(
    cols_per, jr, offsets, tables_at, cols_ref, tab_ref, out_ref, lines, wide, prods
):
    n = cols_ref.shape[0]
    half = cols_ref.shape[2] // jr
    nz = cols_ref.shape[3]
    full = n * half
    step = pl.program_id(0)
    tables = tab_ref.shape[0]
    angles = tab_ref.shape[1]
    lags = tab_ref.shape[2]

    @pl.when(step == 0)
    def _():
        for f in range(2):
            for j in range(jr):
                for t in range(full // nz):
                    per = nz // half
                    block = cols_ref[pl.ds(t * per, per), f, pl.ds(j * half, half), :]
                    block = block.reshape(nz, nz).astype(F32)
                    lines[f, j, :, pl.ds(t * nz, nz)] = block.T
        lag = lax.broadcasted_iota(jnp.int32, (lags, lags * 8), 0)
        col = lax.broadcasted_iota(jnp.int32, (lags, lags * 8), 1)
        spread = jnp.where(col // 8 == lag, 1.0, 0.0).astype(jnp.bfloat16)
        flat = tab_ref[...].reshape(tables * angles, lags)
        wide[...] = jnp.dot(flat, spread, preferred_element_type=F32).astype(jnp.bfloat16)

    me = lax.axis_index("gx")
    z0 = lax.rem(me * cols_per, nz)
    x_of = lax.broadcasted_iota(jnp.int32, (8, full), 1)
    ta = tables * angles
    sub = lax.broadcasted_iota(jnp.int32, (8, ta), 0)
    row_c = lax.rem(lax.broadcasted_iota(jnp.int32, (angles * 8, lags * 8), 0), 8)
    col_c = lax.rem(lax.broadcasted_iota(jnp.int32, (angles * 8, lags * 8), 1), 8)
    diagonal = row_c == col_c
    lane_ta = lax.broadcasted_iota(jnp.int32, (angles, 8, ta), 2)
    row_a = lax.broadcasted_iota(jnp.int32, (angles, 8, ta), 0)
    weights = []
    for q in range(2):
        row0 = z0 + step * 16 + q * 8
        chosen = jnp.zeros((8, ta), jnp.int32)
        for c in range(8):
            chosen = jnp.where(sub == c, tables_at[row0 + c], chosen)
        wanted = (chosen * angles)[None] + row_a
        pick = jnp.where(lane_ta == wanted, 1.0, 0.0).reshape(angles * 8, ta)
        dense = jnp.dot(pick.astype(jnp.bfloat16), wide[...], preferred_element_type=F32)
        weights.append(jnp.where(diagonal, dense, 0.0).astype(jnp.bfloat16))

    for j in range(jr):
        results = []
        for q in range(2):
            row0 = pl.multiple_of(z0 + step * 16 + q * 8, 8)
            source = lines[0, j, pl.ds(row0, 8), :]
            receiver = lines[1, j, pl.ds(row0, 8), :]
            slot = j * 2 + q
            for d in range(-LAG_REACH, LAG_REACH):
                reach = abs(d)
                inside = (x_of >= reach) & (x_of < full - reach)
                left = pltpu.roll(source, d % full, axis=1) if d else source
                right = pltpu.roll(receiver, (-d) % full, axis=1) if d else receiver
                product = left * right
                prods[slot, d + LAG_REACH] = jnp.where(inside, product, 0.0) if d else product
            lagged = jnp.concatenate(
                [prods[slot, offsets[h] + LAG_REACH] for h in range(lags)], axis=0
            ).astype(jnp.bfloat16)
            total = jnp.dot(weights[q], lagged, preferred_element_type=F32)
            results.append(total.reshape(angles, 8, full))
        both = jnp.concatenate(results, axis=1)
        out_ref[:, j] = both.astype(jnp.bfloat16)


def local(
    waves_now, waves_prev, epsilon, tilt, azimuth, courant, lag_offsets, table_index, lag_tables
):
    n = lax.axis_size("gx")
    width, ny, nz = epsilon.shape
    half = width // 2
    columns = (ny // 2) * nz
    cols_per = columns // n
    jr = max(1, cols_per // nz)
    full = n * half
    plane = (2, width + 2, ny + 2 * PAD, nz)
    dma = pltpu.SemaphoreType.DMA
    cols = pl.pallas_call(
        functools.partial(wave_kernel, n, jr, cols_per),
        out_shape=jax.ShapeDtypeStruct((n, 2, jr * half, nz), SEND),
        in_specs=[pl.BlockSpec(memory_space=pl.ANY)] * 6,
        out_specs=pl.BlockSpec(memory_space=pltpu.VMEM),
        scratch_shapes=[
            pltpu.VMEM(plane, F32),
            pltpu.VMEM(plane, F32),
            pltpu.VMEM(plane, F32),
            pltpu.VMEM((2, width + 2, ny, nz), F32),
            pltpu.VMEM(plane, F32),
            pltpu.VMEM((width, ny, nz), epsilon.dtype),
            pltpu.VMEM((width, ny, nz), tilt.dtype),
            pltpu.VMEM((width, ny, nz), azimuth.dtype),
            pltpu.VMEM((width, ny, nz), courant.dtype),
            pltpu.VMEM((7, width, ny, nz), F32),
            pltpu.VMEM((2, ny, nz), F32),
            pltpu.VMEM((2, (ny // 2) * half, nz), SEND),
            pltpu.VMEM((STEPS - 1, 2, 2, ny, nz), F32),
            pltpu.VMEM((STEPS, 2, 2, ny, nz), F32),
            dma((7,)),
            dma((STEPS, 2)),
            dma((STEPS, 2)),
            dma((n,)),
            dma((n,)),
        ],
        compiler_params=pltpu.CompilerParams(collective_id=0, has_side_effects=True),
        name="waves",
    )(waves_now, waves_prev, epsilon, tilt, azimuth, courant)

    angles, lags = lag_tables.shape[1:]
    tables = lag_tables.shape[0]
    cz = min(cols_per, nz)
    image = pl.pallas_call(
        functools.partial(image_kernel, cols_per, jr),
        grid=(cz // 16,),
        out_shape=jax.ShapeDtypeStruct((angles, jr, cz, full), jnp.bfloat16),
        in_specs=[
            pl.BlockSpec(memory_space=pltpu.SMEM),
            pl.BlockSpec(memory_space=pltpu.SMEM),
            pl.BlockSpec(memory_space=pltpu.VMEM),
            pl.BlockSpec(memory_space=pltpu.VMEM),
        ],
        out_specs=pl.BlockSpec((angles, jr, 16, full), lambda g: (0, 0, g, 0)),
        scratch_shapes=[
            pltpu.VMEM((2, jr, nz, full), F32),
            pltpu.VMEM((tables * angles, lags * 8), jnp.bfloat16),
            pltpu.VMEM((jr * 2, 2 * LAG_REACH, 8, full), F32),
        ],
        name="image",
    )(lag_offsets, table_index, cols, lag_tables)
    return image.reshape(angles, cols_per, full)


def solution(mesh):
    wave = P(None, ("shot", "gx"), None, None)
    cell = P("gx", None, None)
    return jax.shard_map(
        local,
        mesh=mesh,
        in_specs=(wave, wave, cell, cell, cell, cell, P(), P(), P()),
        out_specs=P(None, ("shot", "gx"), None),
        check_vma=False,
    )
```

profile of v0, /device:TPU:13, one launch (start us, length us, event | category | flops | bytes accessed | tf_op | source)
XLA Modules:
  0.0 46.2 jit_solution(11973077561302816488)
XLA Ops:
  0.0 36.4 %waves.1.cols_ref = f32[16,2,32,128]{3,2,1,0:T(8,128)} custom-call(f32[2,32,64,128]{3,2,1,0:T(8,128)} %now_hbm.1, f32[2,32,64,128]{3,2,1,0:T(8,128)} %prev_hbm.1, bf16[32,64,128]{2,1,0:T(8,128)(2,1)} %eps_hbm.1, bf16[32,64,128]{2,1,0:T(8,128)(2,1)} %tilt_hbm.1, bf16[32,64,128]{2,1,0:T(8,128)(2,1)} %azi_hbm.1, bf16[32,64,128]{2,1,0:T(8,128)(2,1)} %cou_hbm.1), custom_call_target="tpu_custom_call" | custom-call | tf_op jit(solution)/shard_map/waves/pallas_call | solution.py:356
  36.4 9.7 %image.1 = bf16[32,2,128,256]{3,2,1,0:T(8,128)(2,1)} custom-call(s32[32]{0:T(128)} %offsets.1, s32[128]{0:T(128)} %tables_at.1, f32[16,2,32,128]{3,2,1,0:T(8,128)} %waves.1.cols_ref, bf16[4,32,32]{2,1,0:T(8,128)(2,1)} %tab_ref.1), custom_call_target="tpu_custom_call" | custom-call | tf_op jit(solution)/shard_map/image/pallas_call | solution.py:389
where the time goes:
time: 46.3 us; the launch traced here: 46.2 us
  Pallas kernels  46.1 us (100%)
    pallas_call x1, Pallas kernels, local(): pl.pallas_call(functools.partial(wave_kernel, n, jr, cols_per), out_shape...  36.4 us
    pallas_call x1, Pallas kernels, local(): pl.pallas_call(functools.partial(image_kernel, cols_per, jr), grid=(cz //...  9.72 us

commit v1 on v0

--- a/solution.py
+++ b/solution.py
@@ -10,22 +10,20 @@
 LAG_REACH = 16
 PAD = 8
 F32 = jnp.float32
-SEND = jnp.float32
+SEND = jnp.bfloat16
 
 
 def sin_cos(x):
     h = x * 0.5
     h2 = h * h
-    s = h2 * (-1.0 / 39916800.0) + (1.0 / 362880.0)
-    s = s * h2 + (-1.0 / 5040.0)
-    s = s * h2 + (1.0 / 120.0)
-    s = s * h2 + (-1.0 / 6.0)
+    s = h2 * 2.609020676498479e-06 + (-0.00019811149207883466)
+    s = s * h2 + 0.008333088613525165
+    s = s * h2 + (-0.16666660477455342)
     s = s * h2 * h + h
-    c = h2 * (1.0 / 479001600.0) + (-1.0 / 3628800.0)
-    c = c * h2 + (1.0 / 40320.0)
-    c = c * h2 + (-1.0 / 720.0)
-    c = c * h2 + (1.0 / 24.0)
-    c = c * h2 + (-0.5)
+    c = h2 * (-2.607799327383753e-07) + 2.4761934264809493e-05
+    c = c * h2 + (-0.0013888404392126607)
+    c = c * h2 + 0.04166664079116777
+    c = c * h2 + (-0.4999999955092854)
     c = c * h2 + 1.0
     s2 = s + s
     return s2 * c, 1.0 - s2 * s
@@ -33,7 +31,7 @@
 
 def wave_kernel(
     n, jr, cols_per, now_hbm, prev_hbm, eps_hbm, tilt_hbm, azi_hbm, cou_hbm, cols_ref,
-    buf0, buf1, dz, sz, dy, eps, tilt, azi, cou, coef, pair, snap, sendbuf, halo,
+    buf0, buf1, dz, dy, eps, tilt, azi, cou, coef, pair, snap, snap_send, sendbuf, halo,
     in_sems, hs_sems, hr_sems, as_sems, ar_sems,
 ):
     width = eps.shape[0]
@@ -70,13 +68,15 @@
     lax.fori_loop(1, n, greet, 0)
 
     zero_rows = jnp.zeros((2, width + 2, PAD, nz), F32)
-    for ref in (buf0, buf1, dz):
+    for ref in (buf0, buf1):
         ref[:, :, pl.ds(0, PAD), :] = zero_rows
         ref[:, :, pl.ds(PAD + ny, PAD), :] = zero_rows
     zero_plane = jnp.zeros((2, ny, nz), F32)
-    for ref in (buf0, buf1, dz, dy):
-        for plane in (0, width + 1):
+    for plane in (0, width + 1):
+        for ref in (buf0, buf1):
             ref[:, plane, rows, :] = zero_plane
+        for ref in (dz, dy):
+            ref[:, plane] = zero_plane
 
     pl.semaphore_wait(barrier, n - 1)
 
@@ -146,48 +146,52 @@
     for copy in copies[4:]:
         copy.wait()
 
-    lane = lax.broadcasted_iota(jnp.int32, (ny, nz), 1)
-    first = lane == 0
-    last = lane == nz - 1
-
-    def z_values(p):
-        up = jnp.where(last, 0.0, pltpu.roll(p, nz - 1, axis=1))
-        dn = jnp.where(first, 0.0, pltpu.roll(p, 1, axis=1))
-        return up - dn, up + dn
-
-    def z_pass(now, x):
-        for f in range(2):
-            d, s = z_values(now[f, x, rows, :])
-            diff = now[f, x, up_rows, :] - now[f, x, dn_rows, :]
-            dz[f, x, rows, :] = d
-            sz[f, x] = s
-            dy[f, x, rows, :] = diff
+    chunk = 16
+    starts = range(0, ny, chunk)
+
+    def z_shifts(p):
+        lane = lax.broadcasted_iota(jnp.int32, p.shape, 1)
+        up = jnp.where(lane == nz - 1, 0.0, pltpu.roll(p, nz - 1, axis=1))
+        dn = jnp.where(lane == 0, 0.0, pltpu.roll(p, 1, axis=1))
+        return up, dn
+
+    def own_plane(now, prv, x):
+        for y in starts:
+            here = pl.ds(y, chunk)
+            c1, c2, c5, c6 = [coef[k, x - 1, here, :] for k in (1, 2, 5, 6)]
+            for f in range(2):
+                p = now[f, x, pl.ds(PAD + y, chunk), :]
+                pu = now[f, x, pl.ds(PAD + y + 1, chunk), :]
+                pd = now[f, x, pl.ds(PAD + y - 1, chunk), :]
+                before = prv[f, x, pl.ds(PAD + y, chunk), :]
+                up, dn = z_shifts(p)
+                diff = pu - pd
+                yup, ydn = z_shifts(diff)
+                part = c6 * p - before + c1 * (pu + pd)
+                part = part + (c2 * (up + dn) + c5 * (yup - ydn))
+                prv[f, x, pl.ds(PAD + y, chunk), :] = part
+                dz[f, x, here, :] = up - dn
+                dy[f, x, here, :] = diff
 
     def update(now, prv, x):
-        c = [coef[k, x - 1] for k in range(7)]
-        out = []
-        for f in range(2):
-            acc = c[6] * now[f, x, rows, :] - prv[f, x, rows, :]
-            acc += c[0] * (now[f, x + 1, rows, :] + now[f, x - 1, rows, :])
-            acc += c[1] * (now[f, x, up_rows, :] + now[f, x, dn_rows, :])
-            acc += c[2] * sz[f, x]
-            acc += c[3] * (dy[f, x + 1, rows, :] - dy[f, x - 1, rows, :])
-            acc += c[4] * (dz[f, x + 1, rows, :] - dz[f, x - 1, rows, :])
-            acc += c[5] * (dz[f, x, up_rows, :] - dz[f, x, dn_rows, :])
-            out.append(acc)
-        for f in range(2):
-            prv[f, x, rows, :] = out[f]
-        return out
+        for y in starts:
+            here = pl.ds(y, chunk)
+            mid = pl.ds(PAD + y, chunk)
+            c0, c3, c4 = [coef[k, x - 1, here, :] for k in (0, 3, 4)]
+            for f in range(2):
+                acc = prv[f, x, mid, :] + c0 * (now[f, x + 1, mid, :] + now[f, x - 1, mid, :])
+                acc += c3 * (dy[f, x + 1, here, :] - dy[f, x - 1, here, :])
+                acc += c4 * (dz[f, x + 1, here, :] - dz[f, x - 1, here, :])
+                prv[f, x, mid, :] = acc
 
     for step in range(STEPS):
         now, prv = bufs[step % 2], bufs[(step + 1) % 2]
-        z_pass(now, 1)
-        z_pass(now, 2)
-        z_pass(now, 3)
+        for x in (1, 2, 3):
+            own_plane(now, prv, x)
 
         def interior(x, carry, now=now, prv=prv):
             update(now, prv, x)
-            z_pass(now, x + 2)
+            own_plane(now, prv, x + 2)
             return carry
 
         lax.fori_loop(2, width - 1, interior, 0)
@@ -202,15 +206,15 @@
                 for f in range(2):
                     p = halo[step, side, f]
                     now[f, plane, rows, :] = p
-                    d, _ = z_values(p)
-                    dz[f, plane, rows, :] = d
+                    up, dn = z_shifts(p)
+                    dz[f, plane] = up - dn
                 for f in range(2):
-                    dy[f, plane, rows, :] = now[f, plane, up_rows, :] - now[f, plane, dn_rows, :]
-
-            out = update(now, prv, edge)
+                    dy[f, plane] = now[f, plane, up_rows, :] - now[f, plane, dn_rows, :]
+
+            update(now, prv, edge)
             if step < STEPS - 1:
                 for f in range(2):
-                    sendbuf[step, side, f] = out[f]
+                    sendbuf[step, side, f] = prv[f, edge, rows, :]
 
                 @pl.when(has)
                 def _(side=side, step=step):
@@ -235,7 +239,7 @@
     def piece(target, source):
         start = pl.multiple_of(((target * cols_per) // nz) * half, half)
         return pltpu.make_async_remote_copy(
-            src_ref=snap.at[:, pl.ds(start, span), :],
+            src_ref=snap_send.at[:, pl.ds(start, span), :],
             dst_ref=cols_ref.at[source],
             send_sem=as_sems.at[target],
             recv_sem=ar_sems.at[source],
@@ -243,13 +247,16 @@
             device_id_type=pl.DeviceIdType.MESH,
         )
 
+    snap_send[...] = snap[...].astype(SEND)
+
     def send_piece(k, carry):
         piece(lax.rem(me + k, n), me).start()
         return carry
 
-    lax.fori_loop(1, n, send_piece, 0)
+    lax.fori_loop(n // 2, n, send_piece, 0)
+    lax.fori_loop(1, n // 2, send_piece, 0)
     start = pl.multiple_of(((me * cols_per) // nz) * half, half)
-    own = pltpu.make_async_copy(snap.at[:, pl.ds(start, span), :], cols_ref.at[me], in_sems.at[6])
+    own = pltpu.make_async_copy(snap_send.at[:, pl.ds(start, span), :], cols_ref.at[me], in_sems.at[6])
     own.start()
 
     for step in range(STEPS):
@@ -299,7 +306,8 @@
 
     me = lax.axis_index("gx")
     z0 = lax.rem(me * cols_per, nz)
-    x_of = lax.broadcasted_iota(jnp.int32, (8, full), 1)
+    lane = lax.broadcasted_iota(jnp.int32, (8, nz), 1)
+    tiles = full // nz
     ta = tables * angles
     sub = lax.broadcasted_iota(jnp.int32, (8, ta), 0)
     row_c = lax.rem(lax.broadcasted_iota(jnp.int32, (angles * 8, lags * 8), 0), 8)
@@ -318,20 +326,32 @@
         dense = jnp.dot(pick.astype(jnp.bfloat16), wide[...], preferred_element_type=F32)
         weights.append(jnp.where(diagonal, dense, 0.0).astype(jnp.bfloat16))
 
+    def moved(parts, d):
+        if d == 0:
+            return parts
+        turned = [pltpu.roll(part, d % nz, axis=1) for part in parts]
+        zero = jnp.zeros((8, nz), F32)
+        if d > 0:
+            return [
+                jnp.where(lane >= d, turned[t], turned[t - 1] if t else zero)
+                for t in range(tiles)
+            ]
+        return [
+            jnp.where(lane < nz + d, turned[t], turned[t + 1] if t + 1 < tiles else zero)
+            for t in range(tiles)
+        ]
+
     for j in range(jr):
         results = []
         for q in range(2):
             row0 = pl.multiple_of(z0 + step * 16 + q * 8, 8)
-            source = lines[0, j, pl.ds(row0, 8), :]
-            receiver = lines[1, j, pl.ds(row0, 8), :]
+            source = [lines[0, j, pl.ds(row0, 8), pl.ds(t * nz, nz)] for t in range(tiles)]
+            receiver = [lines[1, j, pl.ds(row0, 8), pl.ds(t * nz, nz)] for t in range(tiles)]
             slot = j * 2 + q
             for d in range(-LAG_REACH, LAG_REACH):
-                reach = abs(d)
-                inside = (x_of >= reach) & (x_of < full - reach)
-                left = pltpu.roll(source, d % full, axis=1) if d else source
-                right = pltpu.roll(receiver, (-d) % full, axis=1) if d else receiver
-                product = left * right
-                prods[slot, d + LAG_REACH] = jnp.where(inside, product, 0.0) if d else product
+                left, right = moved(source, d), moved(receiver, -d)
+                for t in range(tiles):
+                    prods[slot, d + LAG_REACH, :, pl.ds(t * nz, nz)] = left[t] * right[t]
             lagged = jnp.concatenate(
                 [prods[slot, offsets[h] + LAG_REACH] for h in range(lags)], axis=0
             ).astype(jnp.bfloat16)
@@ -361,15 +381,15 @@
         scratch_shapes=[
             pltpu.VMEM(plane, F32),
             pltpu.VMEM(plane, F32),
-            pltpu.VMEM(plane, F32),
             pltpu.VMEM((2, width + 2, ny, nz), F32),
-            pltpu.VMEM(plane, F32),
+            pltpu.VMEM((2, width + 2, ny, nz), F32),
             pltpu.VMEM((width, ny, nz), epsilon.dtype),
             pltpu.VMEM((width, ny, nz), tilt.dtype),
             pltpu.VMEM((width, ny, nz), azimuth.dtype),
             pltpu.VMEM((width, ny, nz), courant.dtype),
             pltpu.VMEM((7, width, ny, nz), F32),
             pltpu.VMEM((2, ny, nz), F32),
+            pltpu.VMEM((2, (ny // 2) * half, nz), F32),
             pltpu.VMEM((2, (ny // 2) * half, nz), SEND),
             pltpu.VMEM((STEPS - 1, 2, 2, ny, nz), F32),
             pltpu.VMEM((STEPS, 2, 2, ny, nz), F32),

time: 46.3 us -> 47.3 us (1.022)
  the two profiles are of different devices: /device:TPU:13 before, /device:TPU:0 now
where the time goes in v1:
time: 47.3 us; the launch traced here: 47.2 us
  Pallas kernels  47.2 us (100%)
    pallas_call x1, Pallas kernels, local(): pl.pallas_call(functools.partial(wave_kernel, n, jr, cols_per), out_shape...  37.9 us
    pallas_call x1, Pallas kernels, local(): pl.pallas_call(functools.partial(image_kernel, cols_per, jr), grid=(cz //...  9.34 us

profile of v1, /device:TPU:0, one launch (start us, length us, event | category | flops | bytes accessed | tf_op | source)
XLA Modules:
  0.0 47.2 jit_solution(8986691239779961901)
XLA Ops:
  0.0 37.9 %waves.1.cols_ref = bf16[16,2,32,128]{3,2,1,0:T(8,128)(2,1)} custom-call(f32[2,32,64,128]{3,2,1,0:T(8,128)} %now_hbm.1, f32[2,32,64,128]{3,2,1,0:T(8,128)} %prev_hbm.1, bf16[32,64,128]{2,1,0:T(8,128)(2,1)} %eps_hbm.1, bf16[32,64,128]{2,1,0:T(8,128)(2,1)} %tilt_hbm.1, bf16[32,64,128]{2,1,0:T(8,128)(2,1)} %azi_hbm.1, bf16[32,64,128]{2,1,0:T(8,128)(2,1)} %cou_hbm.1), custom_call_target="tpu_custom_call" | custom-call | tf_op jit(solution)/shard_map/waves/pallas_call | solution.py:376
  37.9 9.3 %image.1 = bf16[32,2,128,256]{3,2,1,0:T(8,128)(2,1)} custom-call(s32[32]{0:T(128)} %offsets.1, s32[128]{0:T(128)} %tables_at.1, bf16[16,2,32,128]{3,2,1,0:T(8,128)(2,1)} %waves.1.cols_ref, bf16[4,32,32]{2,1,0:T(8,128)(2,1)} %tab_ref.1), custom_call_target="tpu_custom_call" | custom-call | tf_op jit(solution)/shard_map/image/pallas_call | solution.py:409

commit v2 on v1

--- a/solution.py
+++ b/solution.py
@@ -31,7 +31,7 @@
 
 def wave_kernel(
     n, jr, cols_per, now_hbm, prev_hbm, eps_hbm, tilt_hbm, azi_hbm, cou_hbm, cols_ref,
-    buf0, buf1, dz, dy, eps, tilt, azi, cou, coef, pair, snap, snap_send, sendbuf, halo,
+    buf0, buf1, dz, dy, part, eps, tilt, azi, cou, coef, pair, snap, snap_send, sendbuf, halo,
     in_sems, hs_sems, hr_sems, as_sems, ar_sems,
 ):
     width = eps.shape[0]
@@ -68,15 +68,15 @@
     lax.fori_loop(1, n, greet, 0)
 
     zero_rows = jnp.zeros((2, width + 2, PAD, nz), F32)
-    for ref in (buf0, buf1):
+    for ref in (buf0, buf1, dz):
         ref[:, :, pl.ds(0, PAD), :] = zero_rows
         ref[:, :, pl.ds(PAD + ny, PAD), :] = zero_rows
     zero_plane = jnp.zeros((2, ny, nz), F32)
     for plane in (0, width + 1):
         for ref in (buf0, buf1):
             ref[:, plane, rows, :] = zero_plane
-        for ref in (dz, dy):
-            ref[:, plane] = zero_plane
+        dz[:, plane, rows, :] = zero_plane
+        dy[:, plane] = zero_plane
 
     pl.semaphore_wait(barrier, n - 1)
 
@@ -155,43 +155,52 @@
         dn = jnp.where(lane == 0, 0.0, pltpu.roll(p, 1, axis=1))
         return up, dn
 
-    def own_plane(now, prv, x):
+    def turns(now, x, y):
+        return [z_shifts(now[f, x, pl.ds(PAD + y, chunk), :]) for f in range(2)]
+
+    def own_rows(now, x, y, turned):
+        here = pl.ds(y, chunk)
+        c1, c2, c6 = [coef[k, x - 1, here, :] for k in (1, 2, 6)]
+        for f in range(2):
+            p = now[f, x, pl.ds(PAD + y, chunk), :]
+            pu = now[f, x, pl.ds(PAD + y + 1, chunk), :]
+            pd = now[f, x, pl.ds(PAD + y - 1, chunk), :]
+            up, dn = turned[f]
+            part[f, x, here, :] = c6 * p + c1 * (pu + pd) + c2 * (up + dn)
+            dz[f, x, pl.ds(PAD + y, chunk), :] = up - dn
+            dy[f, x, here, :] = pu - pd
+
+    def own_plane(now, x):
         for y in starts:
-            here = pl.ds(y, chunk)
-            c1, c2, c5, c6 = [coef[k, x - 1, here, :] for k in (1, 2, 5, 6)]
-            for f in range(2):
-                p = now[f, x, pl.ds(PAD + y, chunk), :]
-                pu = now[f, x, pl.ds(PAD + y + 1, chunk), :]
-                pd = now[f, x, pl.ds(PAD + y - 1, chunk), :]
-                before = prv[f, x, pl.ds(PAD + y, chunk), :]
-                up, dn = z_shifts(p)
-                diff = pu - pd
-                yup, ydn = z_shifts(diff)
-                part = c6 * p - before + c1 * (pu + pd)
-                part = part + (c2 * (up + dn) + c5 * (yup - ydn))
-                prv[f, x, pl.ds(PAD + y, chunk), :] = part
-                dz[f, x, here, :] = up - dn
-                dy[f, x, here, :] = diff
-
-    def update(now, prv, x):
-        for y in starts:
+            own_rows(now, x, y, turns(now, x, y))
+
+    def update(now, prv, x, picked=starts):
+        for y in picked:
             here = pl.ds(y, chunk)
             mid = pl.ds(PAD + y, chunk)
-            c0, c3, c4 = [coef[k, x - 1, here, :] for k in (0, 3, 4)]
+            c0, c3, c4, c5 = [coef[k, x - 1, here, :] for k in (0, 3, 4, 5)]
             for f in range(2):
-                acc = prv[f, x, mid, :] + c0 * (now[f, x + 1, mid, :] + now[f, x - 1, mid, :])
+                acc = part[f, x, here, :] - prv[f, x, mid, :]
+                acc += c0 * (now[f, x + 1, mid, :] + now[f, x - 1, mid, :])
                 acc += c3 * (dy[f, x + 1, here, :] - dy[f, x - 1, here, :])
-                acc += c4 * (dz[f, x + 1, here, :] - dz[f, x - 1, here, :])
+                acc += c4 * (dz[f, x + 1, mid, :] - dz[f, x - 1, mid, :])
+                acc += c5 * (
+                    dz[f, x, pl.ds(PAD + y + 1, chunk), :] - dz[f, x, pl.ds(PAD + y - 1, chunk), :]
+                )
                 prv[f, x, mid, :] = acc
 
     for step in range(STEPS):
         now, prv = bufs[step % 2], bufs[(step + 1) % 2]
         for x in (1, 2, 3):
-            own_plane(now, prv, x)
+            own_plane(now, x)
 
         def interior(x, carry, now=now, prv=prv):
-            update(now, prv, x)
-            own_plane(now, prv, x + 2)
+            turned = turns(now, x + 2, 0)
+            for y in starts:
+                update(now, prv, x, (y,))
+                ahead = turns(now, x + 2, y + chunk) if y + chunk < ny else None
+                own_rows(now, x + 2, y, turned)
+                turned = ahead
             return carry
 
         lax.fori_loop(2, width - 1, interior, 0)
@@ -207,7 +216,7 @@
                     p = halo[step, side, f]
                     now[f, plane, rows, :] = p
                     up, dn = z_shifts(p)
-                    dz[f, plane] = up - dn
+                    dz[f, plane, rows, :] = up - dn
                 for f in range(2):
                     dy[f, plane] = now[f, plane, up_rows, :] - now[f, plane, dn_rows, :]
 
@@ -379,6 +388,7 @@
         in_specs=[pl.BlockSpec(memory_space=pl.ANY)] * 6,
         out_specs=pl.BlockSpec(memory_space=pltpu.VMEM),
         scratch_shapes=[
+            pltpu.VMEM(plane, F32),
             pltpu.VMEM(plane, F32),
             pltpu.VMEM(plane, F32),
             pltpu.VMEM((2, width + 2, ny, nz), F32),

time: 47.3 us -> 42.7 us (0.903)
  Pallas kernels: 47.2 us -> 42.5 us
    pallas_call x1, Pallas kernels: 37.9 us -> 33.2 us  [local(): pl.pallas_call(functools.partial(wave_kernel, n, jr, cols_per), out_shape...]
where the time goes in v2:
time: 42.7 us; the launch traced here: 42.5 us
  Pallas kernels  42.5 us (100%)
    pallas_call x1, Pallas kernels, local(): pl.pallas_call(functools.partial(wave_kernel, n, jr, cols_per), out_shape...  33.2 us
    pallas_call x1, Pallas kernels, local(): pl.pallas_call(functools.partial(image_kernel, cols_per, jr), grid=(cz //...  9.34 us

profile of v2, /device:TPU:0, one launch (start us, length us, event | category | flops | bytes accessed | tf_op | source)
XLA Modules:
  0.0 42.5 jit_solution(2071295410178386875)
XLA Ops:
  0.0 33.2 %waves.1.cols_ref = bf16[16,2,32,128]{3,2,1,0:T(8,128)(2,1)} custom-call(f32[2,32,64,128]{3,2,1,0:T(8,128)} %now_hbm.1, f32[2,32,64,128]{3,2,1,0:T(8,128)} %prev_hbm.1, bf16[32,64,128]{2,1,0:T(8,128)(2,1)} %eps_hbm.1, bf16[32,64,128]{2,1,0:T(8,128)(2,1)} %tilt_hbm.1, bf16[32,64,128]{2,1,0:T(8,128)(2,1)} %azi_hbm.1, bf16[32,64,128]{2,1,0:T(8,128)(2,1)} %cou_hbm.1), custom_call_target="tpu_custom_call" | custom-call | tf_op jit(solution)/shard_map/waves/pallas_call | solution.py:385
  33.2 9.3 %image.1 = bf16[32,2,128,256]{3,2,1,0:T(8,128)(2,1)} custom-call(s32[32]{0:T(128)} %offsets.1, s32[128]{0:T(128)} %tables_at.1, bf16[16,2,32,128]{3,2,1,0:T(8,128)(2,1)} %waves.1.cols_ref, bf16[4,32,32]{2,1,0:T(8,128)(2,1)} %tab_ref.1), custom_call_target="tpu_custom_call" | custom-call | tf_op jit(solution)/shard_map/image/pallas_call | solution.py:419

commit v3 on v2

--- a/solution.py
+++ b/solution.py
@@ -306,7 +306,7 @@
                     per = nz // half
                     block = cols_ref[pl.ds(t * per, per), f, pl.ds(j * half, half), :]
                     block = block.reshape(nz, nz).astype(F32)
-                    lines[f, j, :, pl.ds(t * nz, nz)] = block.T
+                    lines[f, j, :, pl.ds(t * nz, nz)] = block.T.astype(SEND)
         lag = lax.broadcasted_iota(jnp.int32, (lags, lags * 8), 0)
         col = lax.broadcasted_iota(jnp.int32, (lags, lags * 8), 1)
         spread = jnp.where(col // 8 == lag, 1.0, 0.0).astype(jnp.bfloat16)
@@ -315,7 +315,7 @@
 
     me = lax.axis_index("gx")
     z0 = lax.rem(me * cols_per, nz)
-    lane = lax.broadcasted_iota(jnp.int32, (8, nz), 1)
+    lane = lax.broadcasted_iota(jnp.int32, (16, nz), 1)
     tiles = full // nz
     ta = tables * angles
     sub = lax.broadcasted_iota(jnp.int32, (8, ta), 0)
@@ -337,9 +337,9 @@
 
     def moved(parts, d):
         if d == 0:
-            return parts
-        turned = [pltpu.roll(part, d % nz, axis=1) for part in parts]
-        zero = jnp.zeros((8, nz), F32)
+            return [part.astype(F32) for part in parts]
+        turned = [pltpu.roll(part, d % nz, axis=1).astype(F32) for part in parts]
+        zero = jnp.zeros((16, nz), F32)
         if d > 0:
             return [
                 jnp.where(lane >= d, turned[t], turned[t - 1] if t else zero)
@@ -352,15 +352,17 @@
 
     for j in range(jr):
         results = []
+        row0 = pl.multiple_of(z0 + step * 16, 16)
+        source = [lines[0, j, pl.ds(row0, 16), pl.ds(t * nz, nz)] for t in range(tiles)]
+        receiver = [lines[1, j, pl.ds(row0, 16), pl.ds(t * nz, nz)] for t in range(tiles)]
+        for d in range(-LAG_REACH, LAG_REACH):
+            left, right = moved(source, d), moved(receiver, -d)
+            for t in range(tiles):
+                product = left[t] * right[t]
+                for q in range(2):
+                    prods[j * 2 + q, d + LAG_REACH, :, pl.ds(t * nz, nz)] = product[8 * q : 8 * q + 8]
         for q in range(2):
-            row0 = pl.multiple_of(z0 + step * 16 + q * 8, 8)
-            source = [lines[0, j, pl.ds(row0, 8), pl.ds(t * nz, nz)] for t in range(tiles)]
-            receiver = [lines[1, j, pl.ds(row0, 8), pl.ds(t * nz, nz)] for t in range(tiles)]
             slot = j * 2 + q
-            for d in range(-LAG_REACH, LAG_REACH):
-                left, right = moved(source, d), moved(receiver, -d)
-                for t in range(tiles):
-                    prods[slot, d + LAG_REACH, :, pl.ds(t * nz, nz)] = left[t] * right[t]
             lagged = jnp.concatenate(
                 [prods[slot, offsets[h] + LAG_REACH] for h in range(lags)], axis=0
             ).astype(jnp.bfloat16)
@@ -428,7 +430,7 @@
         ],
         out_specs=pl.BlockSpec((angles, jr, 16, full), lambda g: (0, 0, g, 0)),
         scratch_shapes=[
-            pltpu.VMEM((2, jr, nz, full), F32),
+            pltpu.VMEM((2, jr, nz, full), SEND),
             pltpu.VMEM((tables * angles, lags * 8), jnp.bfloat16),
             pltpu.VMEM((jr * 2, 2 * LAG_REACH, 8, full), F32),
         ],

time: 42.7 us -> 41 us (0.960)
  Pallas kernels: 42.5 us -> 40.9 us
    pallas_call x1, Pallas kernels: 9.34 us -> 7.7 us  [local(): pl.pallas_call(functools.partial(image_kernel, cols_per, jr), grid=(cz //...]
where the time goes in v3:
time: 41 us; the launch traced here: 40.9 us
  Pallas kernels  40.9 us (100%)
    pallas_call x1, Pallas kernels, local(): pl.pallas_call(functools.partial(wave_kernel, n, jr, cols_per), out_shape...  33.2 us
    pallas_call x1, Pallas kernels, local(): pl.pallas_call(functools.partial(image_kernel, cols_per, jr), grid=(cz //...  7.7 us

profile of v3, /device:TPU:0, one launch (start us, length us, event | category | flops | bytes accessed | tf_op | source)
XLA Modules:
  0.0 40.9 jit_solution(3767067084708682624)
XLA Ops:
  0.0 33.2 %waves.1.cols_ref = bf16[16,2,32,128]{3,2,1,0:T(8,128)(2,1)} custom-call(f32[2,32,64,128]{3,2,1,0:T(8,128)} %now_hbm.1, f32[2,32,64,128]{3,2,1,0:T(8,128)} %prev_hbm.1, bf16[32,64,128]{2,1,0:T(8,128)(2,1)} %eps_hbm.1, bf16[32,64,128]{2,1,0:T(8,128)(2,1)} %tilt_hbm.1, bf16[32,64,128]{2,1,0:T(8,128)(2,1)} %azi_hbm.1, bf16[32,64,128]{2,1,0:T(8,128)(2,1)} %cou_hbm.1), custom_call_target="tpu_custom_call" | custom-call | tf_op jit(solution)/shard_map/waves/pallas_call | solution.py:387
  33.2 7.7 %image.1 = bf16[32,2,128,256]{3,2,1,0:T(8,128)(2,1)} custom-call(s32[32]{0:T(128)} %offsets.1, s32[128]{0:T(128)} %tables_at.1, bf16[16,2,32,128]{3,2,1,0:T(8,128)(2,1)} %waves.1.cols_ref, bf16[4,32,32]{2,1,0:T(8,128)(2,1)} %tab_ref.1), custom_call_target="tpu_custom_call" | custom-call | tf_op jit(solution)/shard_map/image/pallas_call | solution.py:421
